TPU v7x, 32 devices: a whole 2x2x4 slice. The times are simulated.
32 devices in a mesh: src: 8 (over y, x, core), rcv: 4 (over z).
Axes of the slice: x: 2, y: 2, z: 4, core: 2. Of those that a mesh axis runs over, the one named last changes fastest.
Arguments:
- traces: bfloat16 [256, 128, 512], P('src', 'rcv')
- block_recorded_mask: int32 [8, 4], P('src', 'rcv'), may hold values 0 or 1
- block_live_count: int32 [8, 4], P('src', 'rcv'), may hold values from 256 to 1024, as said below
Outputs:
- deconvolved: float32 [256, 128, 512], P('src', 'rcv')
Inputs may be any that keep to these rules, and one draw needn't show every extreme that they name: `block_live_count`: every block's count lies between a quarter of its 1024 traces and all of them; some block is full in every draw.
All inputs are finite; a program needn't handle non-finite values. No bound on the sum of `block_recorded_mask` on one device may be relied on, other than what follows from the above.
Results may differ from a plain program's by a relative error of at most 0.0003.
Values sent between devices are 32-bit elements; how exact they have to be, the bound alone decides.
A program may use at most 64 MiB of HBM per device.

v0:
```python
import math

import jax
import jax.numpy as jnp
from jax import lax
from jax.sharding import PartitionSpec as P

ITERS = 2


WATER = 0.01


def log_power(real_part, imag_part, length):
    power = (real_part * real_part + imag_part * imag_part) / length
    level = jnp.mean(power, axis=-1, keepdims=True)
    return jnp.log(power + WATER * level + 1e-06)


def robust_weights(logs, trace_present, src_term, rcv_term):
    resid = logs - src_term[:, None, :] - rcv_term[None, :, :]
    square = resid * resid
    padded_spectra = jnp.pad(square, ((0, 0), (0, 0), (1, 1)), mode="edge")
    smooth = 0.25 * padded_spectra[..., :-2] + 0.5 * square + 0.25 * padded_spectra[..., 2:]
    return trace_present[:, :, None] / (1.0 + smooth)


def transform_tables(length, freqs):
    sample = lax.iota(jnp.int32, length)
    bins = lax.iota(jnp.int32, freqs)
    phase = sample[:, None] * bins[None, :] % length
    angle = phase.astype(jnp.float32) * (2.0 * math.pi / length)
    cosine = jnp.cos(angle)
    sine = jnp.sin(angle)
    forward = jnp.concatenate([cosine, -sine], axis=1)
    weight_factor = jnp.where(bins == 0, 1.0, 2.0).astype(jnp.float32) / length
    inverse = jnp.concatenate(
        [cosine.T * weight_factor[:, None], -sine.T * weight_factor[:, None]], axis=0
    )
    forward_high = forward.astype(jnp.bfloat16)
    widened = lax.optimization_barrier(forward_high).astype(jnp.float32)
    forward_low = (forward - widened).astype(jnp.bfloat16)
    return (forward_high, forward_low, inverse)


def body(traces, block_recorded_mask, block_live_count):
    src_rows, rcv_rows, length = traces.shape
    freqs = length // 2
    count = src_rows * rcv_rows
    forward_high, forward_low, inverse = transform_tables(length, freqs)
    local = lax.iota(jnp.int32, count).reshape(src_rows, rcv_rows)
    recorded = block_recorded_mask[0, 0] == 1
    trace_present = ((local < block_live_count[0, 0]) & recorded).astype(jnp.float32)
    flat = traces.reshape(count, length)
    upper = jnp.dot(flat, forward_high, preferred_element_type=jnp.float32)
    spectra = upper + jnp.dot(flat, forward_low, preferred_element_type=jnp.float32)
    real_part = spectra[:, :freqs]
    imag_part = spectra[:, freqs:]
    logs = log_power(real_part, imag_part, length).reshape(src_rows, rcv_rows, freqs)
    src_term = jnp.zeros((src_rows, freqs), jnp.float32)
    rcv_term = jnp.zeros((rcv_rows, freqs), jnp.float32)
    for sweep in range(ITERS):
        weight = robust_weights(logs, trace_present, src_term, rcv_term)
        src_weighted, src_total = lax.psum(
            (jnp.sum(weight * (logs - rcv_term[None, :, :]), axis=1), jnp.sum(weight, axis=1)),
            "rcv",
        )
        rcv_weighted = jnp.sum(weight * (logs - src_term[:, None, :]), axis=0)
        rcv_total = jnp.sum(weight, axis=0)
        summed, totals = lax.psum((rcv_weighted, rcv_total), "src")
        new_rcv = summed / (totals + 1.0)
        src_term = src_weighted / (src_total + 1.0)
        rcv_term = new_rcv
    gain = jnp.exp(-0.5 * (src_term[:, None, :] + rcv_term[None, :, :])).reshape(count, freqs)
    filtered = jnp.concatenate([real_part * gain, imag_part * gain], axis=1)
    output = jnp.dot(
        filtered, inverse, precision=lax.Precision.HIGH, preferred_element_type=jnp.float32
    )
    return output.reshape(src_rows, rcv_rows, length) * trace_present[:, :, None]


def solution(mesh):
    return jax.shard_map(
        body,
        mesh=mesh,
        in_specs=(P("src", "rcv", None), P("src", "rcv"), P("src", "rcv")),
        out_specs=P("src", "rcv", None),
        check_vma=False,
    )
```

profile of v0, /device:TPU:0, one launch (start us, length us, event | category | flops | bytes accessed | tf_op | source)
XLA Modules:
  0.0 216.1 jit_solution(16369489163059285672)
XLA Ops:
  6.5 0.0 copy-start
  6.5 0.0 all-reduce.11.cloned.1.call-start
  6.5 2.1 sine_negate_fusion
  8.6 0.1 fusion.19
  8.7 0.0 copy-done
  8.7 0.8 fusion.43
  9.4 0.8 add_bitcast_fusion
  10.2 0.0 copy-start.1
  10.2 0.2 fusion.33
  10.5 1.1 copy-done.1
  11.6 0.3 add_log_fusion
  11.8 0.3 copy.4
  12.2 0.1 bitcast_multiply_fusion
  12.3 0.2 fusion.42
  13.8 1.6 fusion.40
  15.5 0.0 all-reduce.11.cloned.1.call-update
  15.5 0.0 all-reduce.15.cloned.1.call-start
  15.5 0.7 all-reduce.15.cloned.1.call-update
  16.2 0.0 all-reduce.9.cloned.1.call-start
  16.3 55.4 %all-reduce.11.cloned.1.call-done = (f32[32,256]{1,0:T(8,128)}, f32[32,256]{1,0:T(8,128)}) async-done(((f32[32,256]{1,0:T(8,128)}, f32[32,256]{1,0:T(8,128)}), (f32[32,256]{1,0:T(8,128)}, f32[32,256]{1,0:T(8,128)})) %all-reduce.11.cloned.1.call-update) | async-done | bytes 65552 | tf_op jit(solution)/shard_map/psum | solution.py:70
  71.7 0.8 add_divide_fusion.2
  72.5 35.3 %all-reduce.15.cloned.1.call-done = (f32[32,256]{1,0:T(8,128)}, f32[32,256]{1,0:T(8,128)}) async-done(((f32[32,256]{1,0:T(8,128)}, f32[32,256]{1,0:T(8,128)}), (f32[32,256]{1,0:T(8,128)}, f32[32,256]{1,0:T(8,128)})) %all-reduce.15.cloned.1.call-update) | async-done | bytes 65552 | tf_op jit(solution)/shard_map/psum | solution.py:64
  107.8 0.8 add_divide_fusion.3
  108.6 0.2 subtract_multiply_fusion
  108.8 0.2 fusion.41
  109.0 1.7 fusion.39
  110.7 0.0 all-reduce.9.cloned.1.call-update
  110.8 0.0 copy-start.2
  110.8 0.0 all-reduce.13.cloned.1.call-start
  110.8 3.1 %cosine_multiply_fusion = (f32[256,512]{1,0:T(8,128)}, f32[256,512]{1,0:T(8,128)}) fusion(f32[256]{0:T(256)S(1)} %fusion.36), kind=kLoop, calls=%fused_computation.49 | loop fusion | flops 2228224 | bytes 1049600 | tf_op jit(solution)/shard_map/mul | solution.py:38
  113.9 0.0 all-reduce.13.cloned.1.call-update
  113.9 50.2 %all-reduce.9.cloned.1.call-done = (f32[32,256]{1,0:T(8,128)}, f32[32,256]{1,0:T(8,128)}) async-done(((f32[32,256]{1,0:T(8,128)}, f32[32,256]{1,0:T(8,128)}), (f32[32,256]{1,0:T(8,128)}, f32[32,256]{1,0:T(8,128)})) %all-reduce.9.cloned.1.call-update) | async-done | bytes 65552 | tf_op jit(solution)/shard_map/psum | solution.py:70
  164.1 0.8 add_divide_fusion
  164.9 35.2 %all-reduce.13.cloned.1.call-done = (f32[32,256]{1,0:T(8,128)}, f32[32,256]{1,0:T(8,128)}) async-done(((f32[32,256]{1,0:T(8,128)}, f32[32,256]{1,0:T(8,128)}), (f32[32,256]{1,0:T(8,128)}, f32[32,256]{1,0:T(8,128)})) %all-reduce.13.cloned.1.call-update) | async-done | bytes 65552 | tf_op jit(solution)/shard_map/psum | solution.py:64
  200.1 0.8 add_divide_fusion.1
  200.8 1.1 multiply_exponential_fusion
  202.0 2.6 %copy.5 = f32[1024,256]{0,1:T(8,128)} copy(f32[1024,256]{1,0:T(8,128)} %bitcast.21) | data formatting | bytes 2097152 | tf_op jit(solution)/shard_map/exp | solution.py:74
  204.6 0.0 copy-done.2
  204.6 0.0 copy-start.3
  204.6 0.0 copy-start.4
  204.6 1.6 slice_multiply_fusion.1
  206.2 0.0 copy-done.3
  206.2 0.0 copy-done.4
  206.2 1.9 fusion
  208.1 1.5 broadcast_multiply_fusion
  (3 shorter events, 0.0 us)
Async XLA Ops:
  6.5 2.1 copy-start
  6.5 65.2 %all-reduce.11.cloned.1.call-start = ((), (), s32[]{:S(2)}) async-start(), calls=%async_computation.1 | async-start | bytes 131072 | tf_op jit(solution)/shard_map/psum | solution.py:70
  10.2 1.3 copy-start.1
  15.5 92.3 %all-reduce.15.cloned.1.call-start = ((), (), s32[]{:S(2)}) async-start(), calls=%async_computation.3 | async-start | bytes 131072 | tf_op jit(solution)/shard_map/psum | solution.py:64
  16.2 147.8 %all-reduce.9.cloned.1.call-start = ((), (), s32[]{:S(2)}) async-start(), calls=%async_computation | async-start | bytes 131072 | tf_op jit(solution)/shard_map/psum | solution.py:70
  110.8 93.8 %copy-start.2 = (f32[1024,512]{0,1:T(8,128)S(1)}, f32[1024,512]{0,1:T(8,128)}, u32[]{:S(2)}) copy-start(f32[1024,512]{0,1:T(8,128)} %copy-done.1) | copy-start | bytes 6291460
  110.8 89.3 %all-reduce.13.cloned.1.call-start = ((), (), s32[]{:S(2)}) async-start(), calls=%async_computation.2 | async-start | bytes 131072 | tf_op jit(solution)/shard_map/psum | solution.py:64
  204.6 1.6 copy-start.3
  204.6 1.6 copy-start.4
Sparse Core Ops, SparseCore 0:
  15.6 56.0 all-reduce.10
  74.1 33.7 all-reduce.14
  110.9 53.0 all-reduce.8
  166.3 33.7 all-reduce.12
where the time goes:
time: 217 us; the launch traced here: 216 us
  waiting for transfers between devices  177 us (82%)
  other arithmetic  16.7 us (8%)
  between operations  14.6 us (7%)
  local copies, waits for them, and re-layouts  4.46 us (2%)
  matrix products  3.39 us (2%)
    psum x2, waiting for transfers between devices, body(): summed, totals = lax.psum((rcv_weighted, rcv_total), 'src')  106 us
    psum x2, waiting for transfers between devices, body(): lax.psum((jnp.sum(weight * (logs - rcv_term[None, :, :]), axis=1), jnp.su...  70.5 us
  transfers between devices with their start and end apart: 4, of which 4 were waited for; matrix products, arithmetic and copies ran while one was open for 2% of the time, Pallas kernels for 0%

commit v1 on v0

--- a/solution.py
+++ b/solution.py
@@ -1,14 +1,20 @@
+import functools
 import math
 
 import jax
 import jax.numpy as jnp
+import numpy as np
 from jax import lax
+from jax.experimental import pallas as pl
+from jax.experimental.pallas import tpu as pltpu
 from jax.sharding import PartitionSpec as P
 
 ITERS = 2
-
-
 WATER = 0.01
+LANES = 128
+MESH = pl.DeviceIdType.MESH
+F32 = jnp.float32
+BF16 = jnp.bfloat16
 
 
 def log_power(real_part, imag_part, length):
@@ -43,7 +49,7 @@
     return (forward_high, forward_low, inverse)
 
 
-def body(traces, block_recorded_mask, block_live_count):
+def plain_body(traces, block_recorded_mask, block_live_count):
     src_rows, rcv_rows, length = traces.shape
     freqs = length // 2
     count = src_rows * rcv_rows
@@ -79,7 +85,279 @@
     return output.reshape(src_rows, rcv_rows, length) * trace_present[:, :, None]
 
 
+def split_table(table):
+    table = table.astype(np.float32)
+    high = table.astype(BF16)
+    low = (table - high.astype(np.float32)).astype(BF16)
+    return high, low
+
+
+def kernel_tables(length):
+    half = length // 2
+    sample = np.arange(length)
+    forward, inverse = [], []
+    for parity in (0, 1):
+        bins = np.arange(parity, half, 2)
+        angle = (sample[:, None] * bins[None, :] % length) * (2.0 * math.pi / length)
+        cosine, sine = np.cos(angle), np.sin(angle)
+        forward += [cosine, -sine]
+        factor = np.where(bins == 0, 1.0, 2.0)[:, None] / length
+        inverse.append(np.concatenate([cosine[:half].T * factor, -sine[:half].T * factor], axis=0))
+    return split_table(np.concatenate(forward, axis=1)) + split_table(np.stack(inverse))
+
+
+def weigh(even, odd, present, first, last):
+    even, odd = even * even, odd * odd
+    quarter = even.shape[1]
+    left = jnp.where(first, even, pltpu.roll(odd, 1, 1))
+    right = jnp.where(last, odd, pltpu.roll(even, quarter - 1, 1))
+    smooth_even = 0.25 * left + 0.5 * even + 0.25 * odd
+    smooth_odd = 0.25 * even + 0.5 * odd + 0.25 * right
+    return present / (1.0 + smooth_even), present / (1.0 + smooth_odd)
+
+
+def sweep_kernel(
+    rows, ns, nr, mask_ref, count_ref, x_ref, high_ref, low_ref,
+    spec_ref, src_ref, rcv_ref,
+    logs, acc, s_part, r_part, s_recv, r_recv, s_gath, r_gath,
+    s_ssem, s_rsem, r_ssem, r_rsem, sg_ssem, sg_rsem, rg_ssem, rg_rsem,
+):
+    src_rows, rcv_rows = rows
+    length = x_ref.shape[1]
+    quarter = length // 4
+    half = length // 2
+    ks, kr = src_rows // nr, rcv_rows // ns
+    tile = ks * rcv_rows
+    me_s, me_r = lax.axis_index("src"), lax.axis_index("rcv")
+
+    barrier = pltpu.get_barrier_semaphore()
+    for d in range(1, ns):
+        pl.semaphore_signal(barrier, inc=1, device_id={"src": lax.rem(me_s + d, ns)}, device_id_type=MESH)
+    for d in range(1, nr):
+        pl.semaphore_signal(barrier, inc=1, device_id={"rcv": lax.rem(me_r + d, nr)}, device_id_type=MESH)
+
+    limit = count_ref[0, 0] * jnp.where(mask_ref[0, 0] == 1, 1, 0)
+    shape = (rcv_rows, quarter)
+    row = lax.broadcasted_iota(jnp.int32, shape, 0)
+    lane = lax.broadcasted_iota(jnp.int32, shape, 1)
+    first, last = lane == 0, lane == quarter - 1
+
+    def scatter(it, axis, n, me, part, recv, ssem, rsem):
+        copies = []
+        for d in range(1, n):
+            peer = lax.rem(me + d, n)
+            copy = pltpu.make_async_remote_copy(
+                src_ref=part.at[it, peer], dst_ref=recv.at[it, me],
+                send_sem=ssem.at[it, d], recv_sem=rsem.at[it, me],
+                device_id={axis: peer}, device_id_type=MESH,
+            )
+            copy.start()
+            copies.append(copy)
+        return copies
+
+    def gather(it, axis, n, me, gath, ssem, rsem):
+        copies = []
+        for d in range(1, n):
+            peer = lax.rem(me + d, n)
+            copy = pltpu.make_async_remote_copy(
+                src_ref=gath.at[it, me], dst_ref=gath.at[it, me],
+                send_sem=ssem.at[it, d], recv_sem=rsem.at[it, me],
+                device_id={axis: peer}, device_id_type=MESH,
+            )
+            copy.start()
+            copies.append(copy)
+        return copies
+
+    def arrive(it, axis, n, me, buf, ssem, rsem):
+        for d in range(1, n):
+            peer = lax.rem(me + d, n)
+            pltpu.make_async_remote_copy(
+                src_ref=buf.at[it, peer], dst_ref=buf.at[it, peer],
+                send_sem=ssem.at[it, d], recv_sem=rsem.at[it, peer],
+                device_id={axis: peer}, device_id_type=MESH,
+            ).wait_recv()
+
+    def finish(it, n, me, k, part, recv, gath):
+        recv[it, me] = part[it, me]
+        total = recv[it, 0]
+        for j in range(1, n):
+            total = total + recv[it, j]
+        gath[it, me] = total[:k] / (total[k:] + 1.0)
+
+    sends = []
+    acc[...] = jnp.zeros_like(acc)
+    for it in range(ITERS):
+        def chunk(c, carry, it=it):
+            base = pl.multiple_of(c * tile, tile)
+            if it == 0:
+                x = x_ref[pl.ds(base, tile), :]
+                spec_ref[pl.ds(base, tile), :] = jnp.dot(
+                    x, high_ref[...], preferred_element_type=F32
+                ) + jnp.dot(x, low_ref[...], preferred_element_type=F32)
+            else:
+                terms = src_ref[pl.ds(pl.multiple_of(c * ks, ks), ks), :]
+            sums = [jnp.zeros(shape, F32) for _ in range(4)]
+            for i in range(ks):
+                at = pl.ds(pl.multiple_of(base + i * rcv_rows, rcv_rows), rcv_rows)
+                present = jnp.where(row + (base + i * rcv_rows) < limit, 1.0, 0.0)
+                if it == 0:
+                    powers = []
+                    for parity in (0, 1):
+                        re = spec_ref[at, parity * half : parity * half + quarter]
+                        im = spec_ref[at, parity * half + quarter : (parity + 1) * half]
+                        powers.append((re * re + im * im) * (1.0 / length))
+                    level = jnp.sum(powers[0] + powers[1], axis=1, keepdims=True) * (1.0 / half)
+                    floor = WATER * level + 1e-06
+                    even, odd = jnp.log(powers[0] + floor), jnp.log(powers[1] + floor)
+                    logs[at, :quarter] = even
+                    logs[at, quarter:] = odd
+                    we, wo = weigh(even, odd, present, first, last)
+                    src_even = rcv_even = we * even
+                    src_odd = rcv_odd = wo * odd
+                else:
+                    even, odd = logs[at, :quarter], logs[at, quarter:]
+                    ue, uo = even - terms[i : i + 1, :quarter], odd - terms[i : i + 1, quarter:]
+                    te, to = rcv_ref[:, :quarter], rcv_ref[:, quarter:]
+                    we, wo = weigh(ue - te, uo - to, present, first, last)
+                    src_even, src_odd = we * (even - te), wo * (odd - to)
+                    rcv_even, rcv_odd = we * ue, wo * uo
+                s_part[it, c, i : i + 1, :quarter] = jnp.sum(src_even, axis=0, keepdims=True)
+                s_part[it, c, i : i + 1, quarter:] = jnp.sum(src_odd, axis=0, keepdims=True)
+                s_part[it, c, ks + i : ks + i + 1, :quarter] = jnp.sum(we, axis=0, keepdims=True)
+                s_part[it, c, ks + i : ks + i + 1, quarter:] = jnp.sum(wo, axis=0, keepdims=True)
+                for q, value in enumerate((rcv_even, rcv_odd, we, wo)):
+                    sums[q] = sums[q] + value
+            acc[it, 0, :, :quarter] += sums[0]
+            acc[it, 0, :, quarter:] += sums[1]
+            acc[it, 1, :, :quarter] += sums[2]
+            acc[it, 1, :, quarter:] += sums[3]
+            return carry
+
+        lax.fori_loop(0, nr, chunk, 0)
+        for p in range(ns):
+            r_part[it, p, :kr, :] = acc[it, 0, p * kr : (p + 1) * kr, :]
+            r_part[it, p, kr:, :] = acc[it, 1, p * kr : (p + 1) * kr, :]
+        if it == 0:
+            pl.semaphore_wait(barrier, ns + nr - 2)
+        sends += scatter(it, "rcv", nr, me_r, s_part, s_recv, s_ssem, s_rsem)
+        sends += scatter(it, "src", ns, me_s, r_part, r_recv, r_ssem, r_rsem)
+        arrive(it, "src", ns, me_s, r_recv, r_ssem, r_rsem)
+        finish(it, ns, me_s, kr, r_part, r_recv, r_gath)
+        sends += gather(it, "src", ns, me_s, r_gath, rg_ssem, rg_rsem)
+        arrive(it, "rcv", nr, me_r, s_recv, s_ssem, s_rsem)
+        finish(it, nr, me_r, ks, s_part, s_recv, s_gath)
+        sends += gather(it, "rcv", nr, me_r, s_gath, sg_ssem, sg_rsem)
+        arrive(it, "src", ns, me_s, r_gath, rg_ssem, rg_rsem)
+        for p in range(ns):
+            rcv_ref[p * kr : (p + 1) * kr, :] = r_gath[it, p]
+        arrive(it, "rcv", nr, me_r, s_gath, sg_ssem, sg_rsem)
+        for p in range(nr):
+            src_ref[p * ks : (p + 1) * ks, :] = s_gath[it, p]
+    for copy in sends:
+        copy.wait_send()
+
+
+def filter_kernel(
+    rows, mask_ref, count_ref, spec_ref, src_ref, rcv_ref, high_ref, low_ref, out_ref, upper, lower
+):
+    rcv_rows, quarter = rows[1], spec_ref.shape[1] // 4
+    half = 2 * quarter
+    sources = spec_ref.shape[0] // rcv_rows
+    base = pl.program_id(0) * spec_ref.shape[0]
+    limit = count_ref[0, 0] * jnp.where(mask_ref[0, 0] == 1, 1, 0)
+    row = lax.broadcasted_iota(jnp.int32, (rcv_rows, quarter), 0)
+    for i in range(sources):
+        at = slice(i * rcv_rows, (i + 1) * rcv_rows)
+        alive = row + (base + i * rcv_rows) < limit
+        for parity in (0, 1):
+            cols = slice(parity * quarter, (parity + 1) * quarter)
+            gain = jnp.exp(-0.5 * (src_ref[i : i + 1, cols] + rcv_ref[:, cols]))
+            gain = jnp.where(alive, gain, 0.0)
+            for part in (0, 1):
+                lo = parity * half + part * quarter
+                value = spec_ref[at, lo : lo + quarter] * gain
+                high = value.astype(BF16)
+                upper[at, lo : lo + quarter] = high
+                lower[at, lo : lo + quarter] = (value - high.astype(F32)).astype(BF16)
+
+    def product(parity):
+        cols = slice(parity * half, (parity + 1) * half)
+        big, small = upper[:, cols], lower[:, cols]
+        dot = functools.partial(jnp.dot, preferred_element_type=F32)
+        return dot(big, high_ref[parity]) + (dot(small, high_ref[parity]) + dot(big, low_ref[parity]))
+
+    a, b = product(0), product(1)
+    out_ref[:, :half] = a + b
+    out_ref[:, half:] = a - b
+
+
+def kernel_body(ns, nr, traces, mask, count):
+    src_rows, rcv_rows, length = traces.shape
+    total, half = src_rows * rcv_rows, length // 2
+    ks, kr = src_rows // nr, rcv_rows // ns
+    forward_high, forward_low, inverse_high, inverse_low = kernel_tables(length)
+    flat = traces.reshape(total, length)
+    vmem = pl.BlockSpec(memory_space=pltpu.VMEM)
+    smem = pl.BlockSpec(memory_space=pltpu.SMEM)
+    dma = pltpu.SemaphoreType.DMA
+    spectra, src_term, rcv_term = pl.pallas_call(
+        functools.partial(sweep_kernel, (src_rows, rcv_rows), ns, nr),
+        out_shape=(
+            jax.ShapeDtypeStruct((total, length), F32),
+            jax.ShapeDtypeStruct((src_rows, half), F32),
+            jax.ShapeDtypeStruct((rcv_rows, half), F32),
+        ),
+        in_specs=[smem, smem, vmem, vmem, vmem],
+        out_specs=(vmem, vmem, vmem),
+        scratch_shapes=[
+            pltpu.VMEM((total, half), F32),
+            pltpu.VMEM((ITERS, 2, rcv_rows, half), F32),
+            pltpu.VMEM((ITERS, nr, 2 * ks, half), F32),
+            pltpu.VMEM((ITERS, ns, 2 * kr, half), F32),
+            pltpu.VMEM((ITERS, nr, 2 * ks, half), F32),
+            pltpu.VMEM((ITERS, ns, 2 * kr, half), F32),
+            pltpu.VMEM((ITERS, nr, ks, half), F32),
+            pltpu.VMEM((ITERS, ns, kr, half), F32),
+            dma((ITERS, nr)), dma((ITERS, nr)), dma((ITERS, ns)), dma((ITERS, ns)),
+            dma((ITERS, nr)), dma((ITERS, nr)), dma((ITERS, ns)), dma((ITERS, ns)),
+        ],
+        compiler_params=pltpu.CompilerParams(
+            collective_id=0, has_side_effects=True, vmem_limit_bytes=24 * 1024 * 1024
+        ),
+        name="sweeps",
+    )(mask, count, flat, jnp.asarray(forward_high), jnp.asarray(forward_low))
+    tile = ks * rcv_rows
+    output = pl.pallas_call(
+        functools.partial(filter_kernel, (src_rows, rcv_rows)),
+        grid=(nr,),
+        out_shape=jax.ShapeDtypeStruct((total, length), F32),
+        in_specs=[
+            smem,
+            smem,
+            pl.BlockSpec((tile, length), lambda i: (i, 0)),
+            pl.BlockSpec((ks, half), lambda i: (i, 0)),
+            pl.BlockSpec((rcv_rows, half), lambda i: (0, 0)),
+            pl.BlockSpec((2, half, half), lambda i: (0, 0, 0)),
+            pl.BlockSpec((2, half, half), lambda i: (0, 0, 0)),
+        ],
+        out_specs=pl.BlockSpec((tile, length), lambda i: (i, 0)),
+        scratch_shapes=[pltpu.VMEM((tile, length), BF16), pltpu.VMEM((tile, length), BF16)],
+        compiler_params=pltpu.CompilerParams(vmem_limit_bytes=24 * 1024 * 1024),
+        name="filters",
+    )(mask, count, spectra, src_term, rcv_term, jnp.asarray(inverse_high), jnp.asarray(inverse_low))
+    return output.reshape(src_rows, rcv_rows, length)
+
+
 def solution(mesh):
+    ns, nr = mesh.shape["src"], mesh.shape["rcv"]
+
+    def body(traces, mask, count):
+        src_rows, rcv_rows, length = traces.shape
+        fits = src_rows % (8 * nr) == 0 and rcv_rows % (4 * ns) == 0 and length % (4 * LANES) == 0
+        if fits and ns > 1 and nr > 1:
+            return kernel_body(ns, nr, traces, mask, count)
+        return plain_body(traces, mask, count)
+
     return jax.shard_map(
         body,
         mesh=mesh,

time: 217 us -> 31.2 us (0.14)
  waiting for transfers between devices: 177 us -> 0 us
  Pallas kernels: 0 us -> 26.3 us
  other arithmetic: 16.7 us -> 0 us
  between operations: 14.6 us -> 1.33 us
  matrix products: 3.39 us -> 0 us
    psum x4 -> x0, waiting for transfers between devices: 176 us -> none  [the longest x2 106 us: body(): summed, totals = lax.psum((rcv_weighted, rcv_total), 'src')]
    pallas_call x0 -> x2, Pallas kernels: none -> 26.3 us  [the longest x1 23.3 us: kernel_body(): pl.pallas_call(functools.partial(sweep_kernel, (src_rows, rcv_rows), ns,...]
    mul x6 -> x0, other arithmetic: 6.46 us -> none  [the longest x1 3.06 us: transform_tables(): cosine.T * weight_factor[:, None]]
    reduce_sum x3 -> x0, other arithmetic: 3.56 us -> none  [the longest x2 3.35 us: body(): jnp.sum(weight, axis=1)]
    dot_general x3 -> x0, matrix products: 3.39 us -> none  [the longest x1 1.85 us: body(): jnp.dot(filtered, inverse, precision=lax.Precision.HIGH, preferred_elemen...]
    div x5 -> x0, other arithmetic: 3.15 us -> none  [the longest x2 1.57 us: body(): new_rcv = summed / (totals + 1.0)]
    exp x1 -> x0, local copies, waits for them, and re-layouts: 2.59 us -> none  [body(): jnp.exp(-0.5 * (src_term[:, None, :] + rcv_term[None, :, :]))]
    unnamed x10, local copies, waits for them, and re-layouts: 1.11 us -> 3.31 us
  transfers between devices with their start and end apart: 4 -> 0, of which waited for: 4 -> 0; matrix products, arithmetic and copies ran while one was open for 2% -> 0% of each run, Pallas kernels for 0% -> 0%
where the time goes in v1:
time: 31.2 us; the launch traced here: 30.9 us
  Pallas kernels  26.3 us (84%)
  local copies, waits for them, and re-layouts  3.31 us (11%)
  between operations  1.33 us (4%)
    pallas_call x1, Pallas kernels, kernel_body(): pl.pallas_call(functools.partial(sweep_kernel, (src_rows, rcv_rows), ns,...  23.3 us
    unnamed x10, local copies, waits for them, and re-layouts  3.31 us
    pallas_call x1, Pallas kernels, kernel_body(): pl.pallas_call(functools.partial(filter_kernel, (src_rows, rcv_rows)), gr...  2.94 us

profile of v1, /device:TPU:0, one launch (start us, length us, event | category | flops | bytes accessed | tf_op | source)
XLA Modules:
  0.0 30.9 jit_solution(11216793241095701095)
XLA Ops:
  1.3 0.0 copy-start
  1.3 1.2 %copy-done = bf16[32,32,512]{2,1,0:T(8,128)(2,1)S(1)} copy-done((bf16[32,32,512]{2,1,0:T(8,128)(2,1)S(1)}, bf16[32,32,512]{2,1,0:T(8,128)(2,1)}, u32[]{:S(2)}) %copy-start) | copy-done | bytes 1048600
  2.5 0.0 copy-start.1
  2.5 1.0 %copy-done.1 = bf16[512,512]{1,0:T(8,128)(2,1)S(1)} copy-done((bf16[512,512]{1,0:T(8,128)(2,1)S(1)}, bf16[512,512]{1,0:T(8,128)(2,1)}, u32[]{:S(2)}) %copy-start.1) | copy-done | bytes 524312
  3.6 0.0 copy-start.2
  3.6 1.0 %copy-done.2 = bf16[512,512]{1,0:T(8,128)(2,1)S(1)} copy-done((bf16[512,512]{1,0:T(8,128)(2,1)S(1)}, bf16[512,512]{1,0:T(8,128)(2,1)}, u32[]{:S(2)}) %copy-start.2) | copy-done | bytes 524312
  4.6 0.0 copy-start.3
  4.6 0.0 copy-start.4
  4.6 23.3 %sweeps.1 = (f32[1024,512]{1,0:T(8,128)S(1)}, f32[32,256]{1,0:T(8,128)S(1)}, f32[32,256]{1,0:T(8,128)S(1)}) custom-call(s32[1,1]{1,0:T(1,128)S(6)} %copy.8.mask_ref, s32[1,1]{1,0:T(1,128)S(6)} %copy.9.count_ref, bf16[1024,512]{1,0:T(8,128)(2,1)S(1)} %bitcast.2, bf16[512,512]{1,0:T(8,128)(2,1)S(1)} %copy-done.2, bf16[512,512]{1,0:T(8,128)(2,1)S(1)} %copy-done.1), custom_call_target="tpu_custom_call" | custom-call | tf_op jit(solution)/shard_map/sweeps/pallas_call | solution.py:303
  28.0 0.0 copy-done.3
  28.0 0.0 copy-done.4
  28.0 2.9 %filters.1 = f32[1024,512]{1,0:T(8,128)} custom-call(s32[1,1]{1,0:T(1,128)S(6)} %copy.8.mask_ref, s32[1,1]{1,0:T(1,128)S(6)} %copy.9.count_ref, f32[1024,512]{1,0:T(8,128)S(1)} %get-tuple-element.8.spec_ref, f32[32,256]{1,0:T(8,128)S(1)} %get-tuple-element.9.src_ref, f32[32,256]{1,0:T(8,128)S(1)} %get-tuple-element.10.rcv_ref, ...), custom_call_target="tpu_custom_call" | custom-call | tf_op jit(solution)/shard_map/filters/pallas_call | solution.py:330
Async XLA Ops:
  1.3 1.2 %copy-start = (bf16[32,32,512]{2,1,0:T(8,128)(2,1)S(1)}, bf16[32,32,512]{2,1,0:T(8,128)(2,1)}, u32[]{:S(2)}) copy-start(bf16[32,32,512]{2,1,0:T(8,128)(2,1)} %param.7) | copy-start | bytes 3145732
  2.5 1.0 %copy-start.1 = (bf16[512,512]{1,0:T(8,128)(2,1)S(1)}, bf16[512,512]{1,0:T(8,128)(2,1)}, u32[]{:S(2)}) copy-start(bf16[512,512]{1,0:T(8,128)(2,1)} %constant.9.clone.low_ref) | copy-start | bytes 1572868
  3.6 1.0 %copy-start.2 = (bf16[512,512]{1,0:T(8,128)(2,1)S(1)}, bf16[512,512]{1,0:T(8,128)(2,1)}, u32[]{:S(2)}) copy-start(bf16[512,512]{1,0:T(8,128)(2,1)} %constant.8.clone.high_ref) | copy-start | bytes 1572868
  4.6 23.3 %copy-start.3 = (bf16[2,256,256]{2,1,0:T(8,128)(2,1)S(1)}, bf16[2,256,256]{2,1,0:T(8,128)(2,1)}, u32[]{:S(2)}) copy-start(bf16[2,256,256]{2,1,0:T(8,128)(2,1)} %constant.11.clone.low_ref) | copy-start | bytes 786436
  4.6 23.4 %copy-start.4 = (bf16[2,256,256]{2,1,0:T(8,128)(2,1)S(1)}, bf16[2,256,256]{2,1,0:T(8,128)(2,1)}, u32[]{:S(2)}) copy-start(bf16[2,256,256]{2,1,0:T(8,128)(2,1)} %constant.10.clone.high_ref) | copy-start | bytes 786436

commit v2 on v1

v2 whole, which is shorter than its diff:
```python
import functools
import math

import jax
import jax.numpy as jnp
import numpy as np
from jax import lax
from jax.experimental import pallas as pl
from jax.experimental.pallas import tpu as pltpu
from jax.sharding import PartitionSpec as P

ITERS = 2
WATER = 0.01
LANES = 128
VMEM_BYTES = 64 * 1024 * 1024
ROOM = 44 * 256 * 1024
MESH = pl.DeviceIdType.MESH
F32 = jnp.float32
BF16 = jnp.bfloat16


def log_power(real_part, imag_part, length):
    power = (real_part * real_part + imag_part * imag_part) / length
    level = jnp.mean(power, axis=-1, keepdims=True)
    return jnp.log(power + WATER * level + 1e-06)


def robust_weights(logs, trace_present, src_term, rcv_term):
    resid = logs - src_term[:, None, :] - rcv_term[None, :, :]
    square = resid * resid
    padded_spectra = jnp.pad(square, ((0, 0), (0, 0), (1, 1)), mode="edge")
    smooth = 0.25 * padded_spectra[..., :-2] + 0.5 * square + 0.25 * padded_spectra[..., 2:]
    return trace_present[:, :, None] / (1.0 + smooth)


def transform_tables(length, freqs):
    sample = lax.iota(jnp.int32, length)
    bins = lax.iota(jnp.int32, freqs)
    phase = sample[:, None] * bins[None, :] % length
    angle = phase.astype(jnp.float32) * (2.0 * math.pi / length)
    cosine = jnp.cos(angle)
    sine = jnp.sin(angle)
    forward = jnp.concatenate([cosine, -sine], axis=1)
    weight_factor = jnp.where(bins == 0, 1.0, 2.0).astype(jnp.float32) / length
    inverse = jnp.concatenate(
        [cosine.T * weight_factor[:, None], -sine.T * weight_factor[:, None]], axis=0
    )
    forward_high = forward.astype(jnp.bfloat16)
    widened = lax.optimization_barrier(forward_high).astype(jnp.float32)
    forward_low = (forward - widened).astype(jnp.bfloat16)
    return (forward_high, forward_low, inverse)


def plain_body(traces, block_recorded_mask, block_live_count):
    src_rows, rcv_rows, length = traces.shape
    freqs = length // 2
    count = src_rows * rcv_rows
    forward_high, forward_low, inverse = transform_tables(length, freqs)
    local = lax.iota(jnp.int32, count).reshape(src_rows, rcv_rows)
    recorded = block_recorded_mask[0, 0] == 1
    trace_present = ((local < block_live_count[0, 0]) & recorded).astype(jnp.float32)
    flat = traces.reshape(count, length)
    upper = jnp.dot(flat, forward_high, preferred_element_type=jnp.float32)
    spectra = upper + jnp.dot(flat, forward_low, preferred_element_type=jnp.float32)
    real_part = spectra[:, :freqs]
    imag_part = spectra[:, freqs:]
    logs = log_power(real_part, imag_part, length).reshape(src_rows, rcv_rows, freqs)
    src_term = jnp.zeros((src_rows, freqs), jnp.float32)
    rcv_term = jnp.zeros((rcv_rows, freqs), jnp.float32)
    for sweep in range(ITERS):
        weight = robust_weights(logs, trace_present, src_term, rcv_term)
        src_weighted, src_total = lax.psum(
            (jnp.sum(weight * (logs - rcv_term[None, :, :]), axis=1), jnp.sum(weight, axis=1)),
            "rcv",
        )
        rcv_weighted = jnp.sum(weight * (logs - src_term[:, None, :]), axis=0)
        rcv_total = jnp.sum(weight, axis=0)
        summed, totals = lax.psum((rcv_weighted, rcv_total), "src")
        new_rcv = summed / (totals + 1.0)
        src_term = src_weighted / (src_total + 1.0)
        rcv_term = new_rcv
    gain = jnp.exp(-0.5 * (src_term[:, None, :] + rcv_term[None, :, :])).reshape(count, freqs)
    filtered = jnp.concatenate([real_part * gain, imag_part * gain], axis=1)
    output = jnp.dot(
        filtered, inverse, precision=lax.Precision.HIGH, preferred_element_type=jnp.float32
    )
    return output.reshape(src_rows, rcv_rows, length) * trace_present[:, :, None]


def split_table(table):
    table = table.astype(np.float32)
    high = table.astype(BF16)
    low = (table - high.astype(np.float32)).astype(BF16)
    return high, low


def kernel_tables(length):
    half = length // 2
    sample = np.arange(length)
    forward, inverse = [], []
    for parity in (0, 1):
        bins = np.arange(parity, half, 2)
        angle = (sample[:, None] * bins[None, :] % length) * (2.0 * math.pi / length)
        cosine, sine = np.cos(angle), np.sin(angle)
        forward += [cosine, -sine]
        factor = np.where(bins == 0, 1.0, 2.0)[:, None] / length
        inverse.append(np.concatenate([cosine[:half].T * factor, -sine[:half].T * factor], axis=0))
    return split_table(np.concatenate(forward, axis=1)) + (np.concatenate(split_table(np.stack(inverse))),)


def weigh(even, odd, present, first, last):
    even, odd = even * even, odd * odd
    quarter = even.shape[1]
    left = jnp.where(first, even, pltpu.roll(odd, 1, 1))
    right = jnp.where(last, odd, pltpu.roll(even, quarter - 1, 1))
    smooth_even = 0.25 * left + 0.5 * even + 0.25 * odd
    smooth_odd = 0.25 * even + 0.5 * odd + 0.25 * right
    return present / (1.0 + smooth_even), present / (1.0 + smooth_odd)


def far_first(me, n):
    order = []
    for d in range(n - 1):
        down, up = n - 1 - d, d
        down = down - jnp.where(down <= me, 1, 0)
        up = up + jnp.where(up >= me, 1, 0)
        order.append(jnp.where(2 * me < n, down, up))
    return order + [me]


def sweep_kernel(
    rows, ns, nr, mask_ref, count_ref, x_hbm, high_hbm, low_hbm, inv_hbm,
    spec_hbm, src_ref, rcv_ref, inv_ref,
    spec_ref, x_ref, high_ref, low_ref,
    logs, acc, s_part, r_part, s_recv, r_recv, s_gath, r_gath, in_sem, out_sem,
    s_ssem, s_rsem, r_ssem, r_rsem, sg_ssem, sg_rsem, rg_ssem, rg_rsem,
):
    src_rows, rcv_rows = rows
    length = x_ref.shape[1]
    quarter = length // 4
    half = length // 2
    ks, kr = src_rows // nr, rcv_rows // ns
    tile = ks * rcv_rows
    me_s, me_r = lax.axis_index("src"), lax.axis_index("rcv")
    order = far_first(me_r, nr)

    barrier = pltpu.get_barrier_semaphore()
    for d in range(1, nr):
        pl.semaphore_signal(barrier, inc=1, device_id={"rcv": lax.rem(me_r + d, nr)}, device_id_type=MESH)
    for d in range(1, ns):
        pl.semaphore_signal(barrier, inc=1, device_id={"src": lax.rem(me_s + d, ns)}, device_id_type=MESH)

    loads = [
        pltpu.make_async_copy(high_hbm, high_ref, in_sem.at[nr]),
        pltpu.make_async_copy(low_hbm, low_ref, in_sem.at[nr + 1]),
    ]
    for d in range(nr):
        base = pl.multiple_of(order[d] * tile, tile)
        loads.append(
            pltpu.make_async_copy(x_hbm.at[pl.ds(base, tile)], x_ref.at[d * tile : (d + 1) * tile], in_sem.at[d])
        )
    loads.append(pltpu.make_async_copy(inv_hbm, inv_ref, in_sem.at[nr + 2]))
    for d in (2, 0, 1, *range(3, nr + 3)):
        loads[d].start()

    limit = count_ref[0, 0] * jnp.where(mask_ref[0, 0] == 1, 1, 0)
    shape = (rcv_rows, quarter)
    row = lax.broadcasted_iota(jnp.int32, shape, 0)
    lane = lax.broadcasted_iota(jnp.int32, shape, 1)
    first, last = lane == 0, lane == quarter - 1
    sends, stores = [], []

    def send(it, axis, peer, slot, src, dst, ssem, rsem, me):
        copy = pltpu.make_async_remote_copy(
            src_ref=src, dst_ref=dst, send_sem=ssem.at[it, slot], recv_sem=rsem.at[it, me],
            device_id={axis: peer}, device_id_type=MESH,
        )
        copy.start()
        sends.append(copy)

    def gather(it, axis, n, me, gath, ssem, rsem):
        for d in range(1, n):
            peer = lax.rem(me + d, n)
            send(it, axis, peer, d, gath.at[it, me], gath.at[it, me], ssem, rsem, me)

    def arrive(it, axis, peer, buf, ssem, rsem):
        pltpu.make_async_remote_copy(
            src_ref=buf.at[it, peer], dst_ref=buf.at[it, peer],
            send_sem=ssem.at[it, 0], recv_sem=rsem.at[it, peer],
            device_id={axis: peer}, device_id_type=MESH,
        ).wait_recv()

    def arrive_all(it, axis, n, me, buf, ssem, rsem):
        for d in range(1, n):
            arrive(it, axis, lax.rem(me + d, n), buf, ssem, rsem)

    def finish(it, n, me, k, part, recv, gath):
        recv[it, me] = part[it, me]
        total = recv[it, 0]
        for j in range(1, n):
            total = total + recv[it, j]
        gath[it, me] = total[:k] / (total[k:] + 1.0)

    def finish_src(it):
        arrive_all(it, "rcv", nr, me_r, s_recv, s_ssem, s_rsem)
        finish(it, nr, me_r, ks, s_part, s_recv, s_gath)
        gather(it, "rcv", nr, me_r, s_gath, sg_ssem, sg_rsem)

    def finish_rcv(it):
        arrive_all(it, "src", ns, me_s, r_recv, r_ssem, r_rsem)
        finish(it, ns, me_s, kr, r_part, r_recv, r_gath)
        gather(it, "src", ns, me_s, r_gath, rg_ssem, rg_rsem)

    def collect_rcv(it):
        arrive_all(it, "src", ns, me_s, r_gath, rg_ssem, rg_rsem)
        for p in range(ns):
            rcv_ref[p * kr : (p + 1) * kr, :] = r_gath[it, p]

    def transform(d):
        loads[d + 2].wait()
        at = slice(d * tile, (d + 1) * tile)
        x = x_ref[at, :]
        spec_ref[at, :] = jnp.dot(x, high_ref[...], preferred_element_type=F32) + jnp.dot(
            x, low_ref[...], preferred_element_type=F32
        )

    loads[0].wait()
    loads[1].wait()
    transform(0)
    for it in range(ITERS):
        steps = range(nr) if it == 0 else range(nr - 1, -1, -1)
        for count, d in enumerate(steps):
            chunk = order[d]
            base = chunk * tile
            if it == 0:
                if d + 1 < nr:
                    transform(d + 1)
            else:
                if d < nr - 1:
                    arrive(it - 1, "rcv", chunk, s_gath, sg_ssem, sg_rsem)
                terms = s_gath[it - 1, chunk]
            sums = [None] * 4
            for i in range(ks):
                top = d * tile + i * rcv_rows
                at = slice(top, top + rcv_rows)
                present = jnp.where(row + (base + i * rcv_rows) < limit, 1.0, 0.0)
                if it == 0:
                    powers = []
                    for parity in (0, 1):
                        re = spec_ref[at, parity * half : parity * half + quarter]
                        im = spec_ref[at, parity * half + quarter : (parity + 1) * half]
                        powers.append((re * re + im * im) * (1.0 / length))
                    level = jnp.sum(powers[0] + powers[1], axis=1, keepdims=True) * (1.0 / half)
                    floor = WATER * level + 1e-06
                    even, odd = jnp.log(powers[0] + floor), jnp.log(powers[1] + floor)
                    logs[at, :quarter] = even
                    logs[at, quarter:] = odd
                    we, wo = weigh(even, odd, present, first, last)
                    src_even = rcv_even = we * even
                    src_odd = rcv_odd = wo * odd
                else:
                    even, odd = logs[at, :quarter], logs[at, quarter:]
                    ue, uo = even - terms[i : i + 1, :quarter], odd - terms[i : i + 1, quarter:]
                    te, to = rcv_ref[:, :quarter], rcv_ref[:, quarter:]
                    we, wo = weigh(ue - te, uo - to, present, first, last)
                    src_even, src_odd = we * (even - te), wo * (odd - to)
                    rcv_even, rcv_odd = we * ue, wo * uo
                s_part[it, chunk, i : i + 1, :quarter] = jnp.sum(src_even, axis=0, keepdims=True)
                s_part[it, chunk, i : i + 1, quarter:] = jnp.sum(src_odd, axis=0, keepdims=True)
                s_part[it, chunk, ks + i : ks + i + 1, :quarter] = jnp.sum(we, axis=0, keepdims=True)
                s_part[it, chunk, ks + i : ks + i + 1, quarter:] = jnp.sum(wo, axis=0, keepdims=True)
                for q, value in enumerate((rcv_even, rcv_odd, we, wo)):
                    sums[q] = value if i == 0 else sums[q] + value
            for q in range(4):
                cols = slice((q % 2) * quarter, (q % 2 + 1) * quarter)
                kept = sums[q] if count == 0 else acc[it, q // 2, :, cols] + sums[q]
                acc[it, q // 2, :, cols] = kept
            if it == 0:
                at = slice(d * tile, (d + 1) * tile)
                stores.append(pltpu.make_async_copy(spec_ref.at[at], spec_hbm.at[at], out_sem.at[d]))
                stores[-1].start()
            if it == 0 and count == 0:
                pl.semaphore_wait(barrier, ns + nr - 2)
            if d < nr - 1:
                send(it, "rcv", chunk, d, s_part.at[it, chunk], s_recv.at[it, me_r], s_ssem, s_rsem, me_r)
        for p in range(ns):
            r_part[it, p, :kr, :] = acc[it, 0, p * kr : (p + 1) * kr, :]
            r_part[it, p, kr:, :] = acc[it, 1, p * kr : (p + 1) * kr, :]
        for d in range(1, ns):
            peer = lax.rem(me_s + d, ns)
            send(it, "src", peer, d, r_part.at[it, peer], r_recv.at[it, me_s], r_ssem, r_rsem, me_s)
        if it == 0:
            finish_src(it)
            finish_rcv(it)
        else:
            finish_rcv(it)
            finish_src(it)
        collect_rcv(it)
    loads[nr + 2].wait()
    arrive_all(it, "rcv", nr, me_r, s_gath, sg_ssem, sg_rsem)
    for p in range(nr):
        src_ref[p * ks : (p + 1) * ks, :] = s_gath[it, p]
    for copy in stores:
        copy.wait()
    for copy in sends:
        copy.wait_send()


def filter_kernel(
    rows, nr, mask_ref, count_ref, spec_hbm, src_ref, rcv_ref, inv_ref, out_hbm,
    spec_ref, upper, lower, stage, in_sem, sem,
):
    src_rows, rcv_rows = rows
    quarter = spec_ref.shape[1] // 4
    half = 2 * quarter
    ks = src_rows // nr
    tile = ks * rcv_rows
    order = far_first(lax.axis_index("rcv"), nr)
    limit = count_ref[0, 0] * jnp.where(mask_ref[0, 0] == 1, 1, 0)
    row = lax.broadcasted_iota(jnp.int32, (rcv_rows, quarter), 0)

    loads = []
    for d in range(nr):
        at = slice(d * tile, (d + 1) * tile)
        loads.append(pltpu.make_async_copy(spec_hbm.at[at], spec_ref.at[at], in_sem.at[d]))
        loads[d].start()

    def apply(d):
        loads[d].wait()
        terms = src_ref[pl.ds(pl.multiple_of(order[d] * ks, ks), ks), :]
        for i in range(ks):
            top = d * tile + i * rcv_rows
            at = slice(top, top + rcv_rows)
            alive = row + (order[d] * tile + i * rcv_rows) < limit
            for parity in (0, 1):
                cols = slice(parity * quarter, (parity + 1) * quarter)
                gain = jnp.exp(-0.5 * (terms[i : i + 1, cols] + rcv_ref[:, cols]))
                gain = jnp.where(alive, gain, 0.0)
                for part in (0, 1):
                    lo = parity * half + part * quarter
                    value = spec_ref[at, lo : lo + quarter] * gain
                    high = value.astype(BF16)
                    upper[at, lo : lo + quarter] = high
                    lower[at, lo : lo + quarter] = (value - high.astype(F32)).astype(BF16)

    def product(at, parity):
        cols = slice(parity * half, (parity + 1) * half)
        big, small = upper[at, cols], lower[at, cols]
        dot = functools.partial(jnp.dot, preferred_element_type=F32)
        return dot(big, inv_ref[parity]) + dot(small, inv_ref[parity]) + dot(big, inv_ref[2 + parity])

    copies = []
    apply(0)
    for d in range(nr):
        if d + 1 < nr:
            apply(d + 1)
        at = slice(d * tile, (d + 1) * tile)
        a, b = product(at, 0), product(at, 1)
        stage[at, :half] = a + b
        stage[at, half:] = a - b
        base = pl.multiple_of(order[d] * tile, tile)
        copy = pltpu.make_async_copy(stage.at[at], out_hbm.at[pl.ds(base, tile)], sem.at[d])
        copy.start()
        copies.append(copy)
    for copy in copies:
        copy.wait()


def kernel_body(ns, nr, traces, mask, count):
    src_rows, rcv_rows, length = traces.shape
    total, half = src_rows * rcv_rows, length // 2
    ks, kr = src_rows // nr, rcv_rows // ns
    forward_high, forward_low, inverse = kernel_tables(length)
    flat = traces.reshape(total, length)
    vmem = pl.BlockSpec(memory_space=pltpu.VMEM)
    smem = pl.BlockSpec(memory_space=pltpu.SMEM)
    hbm = pl.BlockSpec(memory_space=pltpu.HBM)
    dma = pltpu.SemaphoreType.DMA
    spectra, src_term, rcv_term, inverse = pl.pallas_call(
        functools.partial(sweep_kernel, (src_rows, rcv_rows), ns, nr),
        out_shape=(
            jax.ShapeDtypeStruct((total, length), F32),
            jax.ShapeDtypeStruct((src_rows, half), F32),
            jax.ShapeDtypeStruct((rcv_rows, half), F32),
            jax.ShapeDtypeStruct(inverse.shape, BF16),
        ),
        in_specs=[smem, smem, hbm, hbm, hbm, hbm],
        out_specs=(hbm, vmem, vmem, vmem),
        scratch_shapes=[
            pltpu.VMEM((total, length), F32),
            pltpu.VMEM((total, length), BF16),
            pltpu.VMEM((length, length), BF16),
            pltpu.VMEM((length, length), BF16),
            pltpu.VMEM((total, half), F32),
            pltpu.VMEM((ITERS, 2, rcv_rows, half), F32),
            pltpu.VMEM((ITERS, nr, 2 * ks, half), F32),
            pltpu.VMEM((ITERS, ns, 2 * kr, half), F32),
            pltpu.VMEM((ITERS, nr, 2 * ks, half), F32),
            pltpu.VMEM((ITERS, ns, 2 * kr, half), F32),
            pltpu.VMEM((ITERS, nr, ks, half), F32),
            pltpu.VMEM((ITERS, ns, kr, half), F32),
            dma((nr + 3,)),
            dma((nr,)),
            dma((ITERS, nr)), dma((ITERS, nr)), dma((ITERS, ns)), dma((ITERS, ns)),
            dma((ITERS, nr)), dma((ITERS, nr)), dma((ITERS, ns)), dma((ITERS, ns)),
        ],
        compiler_params=pltpu.CompilerParams(
            collective_id=0, has_side_effects=True, vmem_limit_bytes=VMEM_BYTES - ROOM
        ),
        name="sweeps",
    )(mask, count, flat, jnp.asarray(forward_high), jnp.asarray(forward_low), jnp.asarray(inverse))
    output = pl.pallas_call(
        functools.partial(filter_kernel, (src_rows, rcv_rows), nr),
        out_shape=jax.ShapeDtypeStruct((total, length), F32),
        in_specs=[smem, smem, hbm, vmem, vmem, vmem],
        out_specs=hbm,
        scratch_shapes=[
            pltpu.VMEM((total, length), F32),
            pltpu.VMEM((total, length), BF16),
            pltpu.VMEM((total, length), BF16),
            pltpu.VMEM((total, length), F32),
            dma((nr,)),
            dma((nr,)),
        ],
        compiler_params=pltpu.CompilerParams(vmem_limit_bytes=VMEM_BYTES - ROOM),
        name="filters",
    )(mask, count, spectra, src_term, rcv_term, inverse)
    return output.reshape(src_rows, rcv_rows, length)


def solution(mesh):
    ns, nr = mesh.shape["src"], mesh.shape["rcv"]

    def body(traces, mask, count):
        src_rows, rcv_rows, length = traces.shape
        fits = src_rows % (8 * nr) == 0 and rcv_rows % (4 * ns) == 0 and length % (4 * LANES) == 0
        if fits and ns > 1 and nr > 1:
            return kernel_body(ns, nr, traces, mask, count)
        return plain_body(traces, mask, count)

    return jax.shard_map(
        body,
        mesh=mesh,
        in_specs=(P("src", "rcv", None), P("src", "rcv"), P("src", "rcv")),
        out_specs=P("src", "rcv", None),
        check_vma=False,
    )
```

time: 31.2 us -> 27.9 us (0.89)
  local copies, waits for them, and re-layouts: 3.31 us -> 0 us
    unnamed x10 -> x0, local copies, waits for them, and re-layouts: 3.31 us -> none
    pallas_call x1, Pallas kernels: 2.94 us -> 3.5 us  [kernel_body(): pl.pallas_call(functools.partial(filter_kernel, (src_rows, rcv_rows), nr)...]
    pallas_call x1, Pallas kernels: 23.3 us -> 22.9 us  [kernel_body(): pl.pallas_call(functools.partial(sweep_kernel, (src_rows, rcv_rows), ns,...]
where the time goes in v2:
time: 27.9 us; the launch traced here: 27.7 us
  Pallas kernels  26.4 us (95%)
  between operations  1.31 us (5%)
    pallas_call x1, Pallas kernels, kernel_body(): pl.pallas_call(functools.partial(sweep_kernel, (src_rows, rcv_rows), ns,...  22.9 us
    pallas_call x1, Pallas kernels, kernel_body(): pl.pallas_call(functools.partial(filter_kernel, (src_rows, rcv_rows), nr)...  3.5 us

profile of v2, /device:TPU:0, one launch (start us, length us, event | category | flops | bytes accessed | tf_op | source)
XLA Modules:
  0.0 27.7 jit_solution(13535058349254706968)
XLA Ops:
  1.3 22.9 %sweeps.1 = (f32[1024,512]{1,0:T(8,128)}, f32[32,256]{1,0:T(8,128)S(1)}, f32[32,256]{1,0:T(8,128)S(1)}, bf16[4,256,256]{2,1,0:T(8,128)(2,1)S(1)}) custom-call(s32[1,1]{1,0:T(1,128)S(6)} %copy.7.mask_ref, s32[1,1]{1,0:T(1,128)S(6)} %copy.8.count_ref, bf16[1024,512]{1,0:T(8,128)(2,1)} %bitcast.2, bf16[512,512]{1,0:T(8,128)(2,1)} %constant.6.clone.high_hbm, ...), custom_call_target="tpu_custom_call" | custom-call | tf_op jit(solution)/shard_map/sweeps/pallas_call | solution.py:379
  24.2 3.5 %filters.1 = f32[1024,512]{1,0:T(8,128)} custom-call(s32[1,1]{1,0:T(1,128)S(6)} %copy.7.mask_ref, s32[1,1]{1,0:T(1,128)S(6)} %copy.8.count_ref, f32[1024,512]{1,0:T(8,128)} %get-tuple-element.9.spec_hbm, f32[32,256]{1,0:T(8,128)S(1)} %get-tuple-element.10.src_ref, f32[32,256]{1,0:T(8,128)S(1)} %get-tuple-element.11.rcv_ref, ...), custom_call_target="tpu_custom_call" | custom-call | tf_op jit(solution)/shard_map/filters/pallas_call | solution.py:412
